TPU v7x, 256 devices: a whole 4x4x8 slice. The times are simulated.
256 devices in a mesh: samp: 8 (over y, core), feat: 32 (over x, z).
Axes of the slice: x: 4, y: 4, z: 8, core: 2. Of those that a mesh axis runs over, the one named last changes fastest.
Arguments:
- samples: bfloat16 [8192, 16384], P('samp', 'feat'), may hold values from -8 to 8
- precision: float32 [128, 8, 128, 128], P('feat'), may hold values from -1.2 to 2
- col_blocks: int32 [128, 8], P('feat'), may hold values from -1 to 127, as said below
Outputs:
- updated: float32 [128, 8, 128, 128], P('feat')
Inputs may be any that keep to these rules, and one draw needn't show every extreme that they name: `col_blocks`: slot 0 of block row j holds j; the other column blocks of a row follow in increasing order, then -1 fills the empty slots. The pattern is symmetric: row j names c exactly when row c names j. Block row j lies on index j // 4 of feat; for two different such indices, at most one block row of the one names a column block of the other, and the block rows of one index name column blocks of at most 16 other indices.
All inputs are finite; a program needn't handle non-finite values.
Results may differ from a plain program's by a relative error of at most 0.0028.
Values may be sent and summed in bfloat16 or wider, within the bound.
A program may use at most 128 MiB of HBM per device.

v0:
```python
import jax
import jax.numpy as jnp
from jax import lax
from jax.sharding import PartitionSpec as P

ITERS = 3


step_size = 0.2
penalty = 0.25


def prox_step(current, gradient, keep_mask, on_diagonal):
    stepped = current - step_size * gradient
    shrunk = jnp.sign(stepped) * jnp.maximum(jnp.abs(stepped) - step_size * penalty, 0.0)
    rooted = 0.5 * (stepped + jnp.sqrt(stepped * stepped + 4.0 * step_size))
    return jnp.where(keep_mask, jnp.where(on_diagonal, rooted, shrunk), jnp.float32(0.0))


def mirror_outbound(flat_gram, send_slot, send_has):
    return jnp.where(
        send_has[:, None, None], jnp.take(flat_gram, send_slot, axis=0), jnp.float32(0.0)
    )


def mirror_inbound(inbound, flat_gram, holder, flat_local, remote):
    from_peer = jnp.take(inbound, holder, axis=0)
    from_self = jnp.take(flat_gram, flat_local, axis=0)
    return jnp.where(remote[:, :, None, None], from_peer, from_self)


def local(samples, precision, col_blocks):
    row_count = samples.shape[0]
    block_rows = precision.shape[0]
    slot_count = precision.shape[1]
    block_size = precision.shape[2]
    flat_count = block_rows * slot_count
    peer_count = lax.axis_size("feat")
    myself = lax.axis_index("feat")
    sample_total = row_count * lax.axis_size("samp")
    filled = col_blocks >= 0
    safe_cols = jnp.where(filled, col_blocks, 0)
    holder = safe_cols // block_rows
    locate = safe_cols % block_rows
    remote = filled & (holder != myself)
    xblocks = samples.reshape(row_count, block_rows, block_size)
    row_ids = myself * block_rows + jnp.arange(block_rows, dtype=jnp.int32)
    peer_ids = jnp.arange(peer_count, dtype=jnp.int32)
    slot_links = (holder[None] == peer_ids[:, None, None]) & remote[None]
    linked = jnp.any(slot_links, axis=2)
    has_link = jnp.any(linked, axis=1)
    source_row = jnp.argmax(linked, axis=1)
    outgoing = jnp.where(
        has_link[None, :, None], jnp.take(xblocks, source_row, axis=1), jnp.zeros((), samples.dtype)
    )
    flat_links = slot_links.reshape(peer_count, flat_count)
    send_slot = jnp.argmax(flat_links, axis=1)
    send_has = jnp.any(flat_links, axis=1)
    matching = col_blocks[locate] == row_ids[:, None, None]
    mate_slot = jnp.argmax(matching, axis=2)
    flat_local = locate * slot_count + mate_slot
    identity_mask = jnp.eye(block_size, dtype=bool)
    on_diagonal = (col_blocks == row_ids[:, None])[:, :, None, None] & identity_mask[None, None]
    keep_mask = filled[:, :, None, None]
    arrived = lax.all_to_all(outgoing, "feat", split_axis=1, concat_axis=1, tiled=True)
    joined = jnp.concatenate([arrived, xblocks], axis=1)
    source_index = jnp.where(remote, holder, peer_count + locate)
    stacked = jnp.take(joined, source_index, axis=1)
    current = jnp.where(keep_mask, precision, jnp.float32(0.0))
    weights = current.astype(jnp.bfloat16)
    for iteration in range(ITERS):
        running = jnp.einsum("rlkb,lkab->rla", stacked, weights, preferred_element_type=jnp.float32)
        projected = running.astype(jnp.bfloat16)
        partial_gram = jnp.einsum(
            "rla,rlkb->lkab", projected, stacked, preferred_element_type=jnp.float32
        )
        gram_blocks = lax.psum(partial_gram, "samp") / sample_total
        flat_gram = gram_blocks.reshape(flat_count, block_size, block_size)
        inbound = lax.all_to_all(
            mirror_outbound(flat_gram, send_slot, send_has),
            "feat",
            split_axis=0,
            concat_axis=0,
            tiled=True,
        )
        mirror = mirror_inbound(inbound, flat_gram, holder, flat_local, remote)
        gradient = 0.5 * (gram_blocks + jnp.swapaxes(mirror, 2, 3))
        current = prox_step(current, gradient, keep_mask, on_diagonal)
        weights = current.astype(jnp.bfloat16)
    return current


def solution(mesh):
    return jax.shard_map(
        local,
        mesh=mesh,
        in_specs=(P("samp", "feat"), P("feat", None, None, None), P("feat", None)),
        out_specs=P("feat", None, None, None),
        check_vma=False,
    )
```

profile of v0, /device:TPU:1, one launch (start us, length us, event | category | flops | bytes accessed | tf_op | source)
XLA Modules:
  0.0 748.8 jit_solution(2308110228360900354)
XLA Ops:
  13.7 4.8 gather_fusion
  18.5 7.6 %select_bitcast_fusion = bf16[1024,32,128]{2,0,1:T(8,128)(2,1)} fusion(bf16[32,1024,128]{2,1,0:T(8,128)(2,1)} %gather_fusion, pred[32]{0:T(512)(128)(4,1)S(1)} %get-tuple-element.13, pred[32]{0:T(512)(128)(4,1)S(1)} %compare_and_fusion.3), kind=kLoop, calls=%fused_computation.25 | loop fusion | flops 8388608 | bytes 16777280 | tf_op jit(solution)/shard_map/jit(_where)/select_n | solution.py:53
  26.0 12.1 %all-to-all-start = ((bf16[1024,32,128]{2,0,1:T(8,128)(2,1)}), bf16[1024,32,128]{2,0,1:T(8,128)(2,1)}, u32[]{:S(2)}, u32[]{:S(2)}) async-start(bf16[1024,32,128]{2,0,1:T(8,128)(2,1)} %select_bitcast_fusion), calls=%async_computation | async-start | bytes 16777216 | tf_op jit(solution)/shard_map/all_to_all | solution.py:65
  40.2 186.1 %all-to-all-done = bf16[1024,32,128]{2,0,1:T(8,128)(2,1)} async-done(((bf16[1024,32,128]{2,0,1:T(8,128)(2,1)}), bf16[1024,32,128]{2,0,1:T(8,128)(2,1)}, u32[]{:S(2)}, u32[]{:S(2)}) %all-to-all-start) | async-done | bytes 8388640 | tf_op jit(solution)/shard_map/all_to_all | solution.py:65
  226.3 8.9 %pad_maximum_fusion = bf16[1024,36,128]{2,0,1:T(8,128)(2,1)} fusion(bf16[1024,4,128]{2,0,1:T(8,128)(2,1)S(1)} %copy.39, bf16[1024,32,128]{2,0,1:T(8,128)(2,1)} %all-to-all-done), kind=kLoop, calls=%fused_computation.12 | loop fusion | flops 4718592 | bytes 18874368 | tf_op jit(solution)/shard_map/concatenate | solution.py:66
  235.3 8.6 %gather_fusion.1 = bf16[32,1024,128]{2,1,0:T(8,128)(2,1)} fusion(bf16[1024,36,128]{2,0,1:T(8,128)(2,1)} %pad_maximum_fusion, s32[1024]{0:T(1024)S(1)} %pad_clamp_fusion.4), kind=kCustom, calls=%fused_computation.10 | custom fusion | bytes 16777344 | tf_op jit(solution)/shard_map/jit(_take)/gather | solution.py:68
  243.9 11.3 %copy.41 = bf16[4,8,1024,128]{2,3,1,0:T(8,128)(2,1)} copy(bf16[4,8,1024,128]{3,2,1,0:T(8,128)(2,1)} %bitcast.129) | data formatting | bytes 16777216 | tf_op jit(solution)/shard_map/jit(_take)/gather | solution.py:68
  255.2 10.8 %fusion.23 = f32[4,8,128,128]{2,3,1,0:T(8,128)} fusion(bf16[4,8,1024,128]{2,3,1,0:T(8,128)(2,1)} %copy.41, pred[4,8]{1,0:T(4,128)(4,1)S(1)} %get-tuple-element.24, f32[4,8,128,128]{2,3,1,0:T(8,128)S(1)} %copy.37, pred[4,8]{1,0:T(4,128)(4,1)S(1)} %get-tuple-element.26), kind=kOutput, calls=%fused_computation.52 | convolution fusion | flops 2156920832 | bytes 12582976 | tf_op jit(solution)/shard_map/rla,rlkb->lkab/dot_general | solution.py:74
  267.0 74.5 %all-reduce.4.cloned.1.call-done = f32[4,8,128,128]{2,3,1,0:T(8,128)} async-done(((f32[4,8,128,128]{2,3,1,0:T(8,128)}), f32[4,8,128,128]{2,3,1,0:T(8,128)}) %all-reduce.4.cloned.1.call-update) | async-done | bytes 2097168 | tf_op jit(solution)/shard_map/psum | solution.py:77
  351.8 9.7 %all-to-all-start.1 = ((f32[32,128,128]{2,1,0:T(8,128)}), f32[32,128,128]{2,1,0:T(8,128)}, u32[]{:S(2)}, u32[]{:S(2)}) async-start(f32[32,128,128]{2,1,0:T(8,128)} %select_select_fusion.5), calls=%async_computation.1 | async-start | bytes 4194304 | tf_op jit(solution)/shard_map/all_to_all | solution.py:79
  363.9 46.0 %all-to-all-done.1 = f32[32,128,128]{2,1,0:T(8,128)} async-done(((f32[32,128,128]{2,1,0:T(8,128)}), f32[32,128,128]{2,1,0:T(8,128)}, u32[]{:S(2)}, u32[]{:S(2)}) %all-to-all-start.1) | async-done | bytes 2097184 | tf_op jit(solution)/shard_map/all_to_all | solution.py:79
  413.4 5.9 fusion.12
  419.4 11.4 %fusion.28 = f32[4,8,128,128]{2,3,1,0:T(8,128)} fusion(bf16[4,8,1024,128]{2,3,1,0:T(8,128)(2,1)} %copy.41, pred[4,8]{1,0:T(4,128)(4,1)S(1)} %get-tuple-element.24, f32[4,8,128,128]{2,3,1,0:T(8,128)} %fusion.12), kind=kOutput, calls=%fused_computation.53 | convolution fusion | flops 2156920832 | bytes 12582944 | tf_op jit(solution)/shard_map/rla,rlkb->lkab/dot_general | solution.py:74
  430.8 69.9 %all-reduce.6.cloned.1.call-done = f32[4,8,128,128]{2,3,1,0:T(8,128)} async-done(((f32[4,8,128,128]{2,3,1,0:T(8,128)}), f32[4,8,128,128]{2,3,1,0:T(8,128)}) %all-reduce.6.cloned.1.call-update) | async-done | bytes 2097168 | tf_op jit(solution)/shard_map/psum | solution.py:77
  511.0 9.7 %all-to-all-start.2 = ((f32[32,128,128]{2,1,0:T(8,128)}), f32[32,128,128]{2,1,0:T(8,128)}, u32[]{:S(2)}, u32[]{:S(2)}) async-start(f32[32,128,128]{2,1,0:T(8,128)} %select_select_fusion.3), calls=%async_computation.2 | async-start | bytes 4194304 | tf_op jit(solution)/shard_map/all_to_all | solution.py:79
  522.9 46.2 %all-to-all-done.2 = f32[32,128,128]{2,1,0:T(8,128)} async-done(((f32[32,128,128]{2,1,0:T(8,128)}), f32[32,128,128]{2,1,0:T(8,128)}, u32[]{:S(2)}, u32[]{:S(2)}) %all-to-all-start.2) | async-done | bytes 2097184 | tf_op jit(solution)/shard_map/all_to_all | solution.py:79
  572.7 6.5 fusion.13
  579.2 11.5 %fusion.33 = f32[4,8,128,128]{2,3,1,0:T(8,128)} fusion(bf16[4,8,1024,128]{2,3,1,0:T(8,128)(2,1)} %copy.41, pred[4,8]{1,0:T(4,128)(4,1)S(1)} %get-tuple-element.24, f32[4,8,128,128]{2,3,1,0:T(8,128)} %fusion.13), kind=kOutput, calls=%fused_computation.54 | convolution fusion | flops 2156920832 | bytes 12582944 | tf_op jit(solution)/shard_map/rla,rlkb->lkab/dot_general | solution.py:74
  590.7 69.9 %all-reduce.8.cloned.1.call-done = f32[4,8,128,128]{2,3,1,0:T(8,128)} async-done(((f32[4,8,128,128]{2,3,1,0:T(8,128)}), f32[4,8,128,128]{2,3,1,0:T(8,128)}) %all-reduce.8.cloned.1.call-update) | async-done | bytes 2097168 | tf_op jit(solution)/shard_map/psum | solution.py:77
  664.2 3.7 gather_fusion.9
  671.1 9.7 %all-to-all-start.3 = ((f32[32,128,128]{2,1,0:T(8,128)}), f32[32,128,128]{2,1,0:T(8,128)}, u32[]{:S(2)}, u32[]{:S(2)}) async-start(f32[32,128,128]{2,1,0:T(8,128)} %select_select_fusion.1), calls=%async_computation.3 | async-start | bytes 4194304 | tf_op jit(solution)/shard_map/all_to_all | solution.py:79
  685.7 43.5 %all-to-all-done.3 = f32[32,128,128]{2,1,0:T(8,128)} async-done(((f32[32,128,128]{2,1,0:T(8,128)}), f32[32,128,128]{2,1,0:T(8,128)}, u32[]{:S(2)}, u32[]{:S(2)}) %all-to-all-start.3) | async-done | bytes 2097184 | tf_op jit(solution)/shard_map/all_to_all | solution.py:79
  729.2 3.6 gather_fusion.10
  732.8 6.5 fusion.14
  (63 shorter events, 57.2 us)
Async XLA Ops:
  26.0 200.3 %all-to-all-start = ((bf16[1024,32,128]{2,0,1:T(8,128)(2,1)}), bf16[1024,32,128]{2,0,1:T(8,128)(2,1)}, u32[]{:S(2)}, u32[]{:S(2)}) async-start(bf16[1024,32,128]{2,0,1:T(8,128)(2,1)} %select_bitcast_fusion), calls=%async_computation | async-start | bytes 16777216 | tf_op jit(solution)/shard_map/all_to_all | solution.py:65
  38.1 303.4 %all-reduce.4.cloned.1.call-start = ((), (), s32[]{:S(2)}) async-start(), calls=%async_computation.4 | async-start | bytes 4194304 | tf_op jit(solution)/shard_map/psum | solution.py:77
  40.2 215.0 %copy-start = (f32[4,8,128,128]{2,3,1,0:T(8,128)}, f32[4,8,128,128]{2,3,1,0:T(8,128)S(1)}, u32[]{:S(2)}) copy-start(f32[4,8,128,128]{2,3,1,0:T(8,128)S(1)} %copy.37) | copy-start | bytes 6291460
  351.8 58.1 %all-to-all-start.1 = ((f32[32,128,128]{2,1,0:T(8,128)}), f32[32,128,128]{2,1,0:T(8,128)}, u32[]{:S(2)}, u32[]{:S(2)}) async-start(f32[32,128,128]{2,1,0:T(8,128)} %select_select_fusion.5), calls=%async_computation.1 | async-start | bytes 4194304 | tf_op jit(solution)/shard_map/all_to_all | solution.py:79
  361.5 139.2 %all-reduce.6.cloned.1.call-start = ((), (), s32[]{:S(2)}) async-start(), calls=%async_computation.5 | async-start | bytes 4194304 | tf_op jit(solution)/shard_map/psum | solution.py:77
  363.9 49.5 %copy-start.1 = (f32[4,8,128,128]{2,3,1,0:T(8,128)S(1)}, f32[4,8,128,128]{2,3,1,0:T(8,128)}, u32[]{:S(2)}) copy-start(f32[4,8,128,128]{2,3,1,0:T(8,128)} %copy-done) | copy-start | bytes 6291460
  511.0 58.1 %all-to-all-start.2 = ((f32[32,128,128]{2,1,0:T(8,128)}), f32[32,128,128]{2,1,0:T(8,128)}, u32[]{:S(2)}, u32[]{:S(2)}) async-start(f32[32,128,128]{2,1,0:T(8,128)} %select_select_fusion.3), calls=%async_computation.2 | async-start | bytes 4194304 | tf_op jit(solution)/shard_map/all_to_all | solution.py:79
  520.7 139.9 %all-reduce.8.cloned.1.call-start = ((), (), s32[]{:S(2)}) async-start(), calls=%async_computation.6 | async-start | bytes 4194304 | tf_op jit(solution)/shard_map/psum | solution.py:77
  522.9 49.8 %copy-start.3 = (f32[4,8,128,128]{2,3,1,0:T(8,128)S(1)}, f32[4,8,128,128]{2,3,1,0:T(8,128)}, u32[]{:S(2)}) copy-start(f32[4,8,128,128]{2,3,1,0:T(8,128)} %all-reduce.6.cloned.1.call-done) | copy-start | bytes 6291460
  671.1 58.1 %all-to-all-start.3 = ((f32[32,128,128]{2,1,0:T(8,128)}), f32[32,128,128]{2,1,0:T(8,128)}, u32[]{:S(2)}, u32[]{:S(2)}) async-start(f32[32,128,128]{2,1,0:T(8,128)} %select_select_fusion.1), calls=%async_computation.3 | async-start | bytes 4194304 | tf_op jit(solution)/shard_map/all_to_all | solution.py:79
  685.7 47.1 %copy-start.2 = (f32[4,8,128,128]{2,3,1,0:T(8,128)S(1)}, f32[4,8,128,128]{2,3,1,0:T(8,128)}, u32[]{:S(2)}) copy-start(f32[4,8,128,128]{2,3,1,0:T(8,128)} %all-reduce.8.cloned.1.call-done) | copy-start | bytes 6291460
Sparse Core Ops, SparseCore 0:
  266.1 75.3 all-reduce.3
  430.9 69.7 all-reduce.5
  590.8 69.7 all-reduce.7
where the time goes:
time: 752 us; the launch traced here: 749 us
  waiting for transfers between devices  536 us (71%)
  local copies, waits for them, and re-layouts  66.5 us (9%)
  other arithmetic  57.6 us (8%)
  starting transfers between devices  41.6 us (6%)
  matrix products  33.7 us (4%)
  between operations  13.3 us (2%)
    psum x3, waiting for transfers between devices, local(): gram_blocks = lax.psum(partial_gram, 'samp') / sample_total  214 us
    all_to_all x1, waiting for transfers between devices, local(): lax.all_to_all(outgoing, 'feat', split_axis=1, concat_axis=1, tiled=True)  186 us
    all_to_all x3, waiting for transfers between devices, local(): lax.all_to_all(mirror_outbound(flat_gram, send_slot, send_has), 'feat', s...  136 us
    dot_general x3, matrix products, local(): jnp.einsum('rla,rlkb->lkab', projected, stacked, preferred_element_type=j...  33.7 us
    all_to_all x3, starting transfers between devices, local(): lax.all_to_all(mirror_outbound(flat_gram, send_slot, send_has), 'feat', s...  29 us
    gather x2, local copies, waits for them, and re-layouts, local(): stacked = jnp.take(joined, source_index, axis=1)  19.9 us
    select_n x3, other arithmetic, prox_step(): jnp.where(keep_mask, jnp.where(on_diagonal, rooted, shrunk), jnp.float32(...  19 us
  transfers between devices with their start and end apart: 7, of which 7 were waited for; matrix products, arithmetic and copies ran while one was open for 2% of the time, Pallas kernels for 0%

commit v1 on v0

v1 whole, which is shorter than its diff:
```python
import functools

import jax
import jax.numpy as jnp
from jax import lax
from jax.experimental import pallas as pl
from jax.experimental.pallas import tpu as pltpu
from jax.sharding import PartitionSpec as P

ITERS = 3
STEP = 0.2
SHRINK = 0.2 * 0.25
NX, NZ, NY, NC = 4, 8, 4, 2
NS = NY * NC
NF = NX * NZ
BR, SL, BK = 4, 8, 128
NBK = BR * SL
CH = BK // NS
ROWS = 1024
F32, BF16 = jnp.float32, jnp.bfloat16
MESH = pl.DeviceIdType.MESH

POOL, FLIP, LOCAL, MATE, PEER, FILLED, LINK, PICK = range(8)
SOURCES = ((0, True, True), (1, True, True), (1, False, False), (2, True, True), (2, False, False),
           (3, True, True), (3, False, False), (4, True, False))


def kernel(tab, x_hbm, prec, out, pool, stage, stk, wt, yt, vv, tile, oc, ub, uf, sb, own, yb, yr, uc, ms, mx, mz, mloc,
           wc, wg, og, loc_sem, zs_sem, zr_sem, xs_sem, xr_sem, bs_sem, br_sem, ys_sem, yr_sem, as_sem, ar_sem,
           ms_sem, mr_sem, gs_sem, gr_sem, hs_sem, hr_sem):
    samp, feat = lax.axis_index("samp"), lax.axis_index("feat")
    y, c = samp // NC, samp % NC
    x, z = feat // NZ, feat % NZ

    def at_x(d):
        return (x + d) % NX

    def at_z(d):
        return (z + d) % NZ

    def at_y(d):
        return (y + d) % NY

    def dev(yy, cc, xx, zz):
        return (yy * NC + cc, xx * NZ + zz)

    def remote(src, dst, ssem, rsem, device):
        return pltpu.make_async_remote_copy(src_ref=src, dst_ref=dst, send_sem=ssem, recv_sem=rsem, device_id=device,
                                            device_id_type=MESH)

    barrier = pltpu.get_barrier_semaphore()
    peers = ([dev(y, c, at_x(d), z) for d in range(1, NX)] + [dev(y, c, x, at_z(d)) for d in range(1, NZ)]
             + [dev(at_y(d), c, x, z) for d in range(1, NY)] + [dev(y, 1 - c, x, z)])
    loads = [pltpu.make_async_copy(x_hbm.at[:, pl.ds(r * BK, BK)], pool.at[z * BR + r], loc_sem.at[r]) for r in range(BR)]
    for load in loads:
        load.start()
    for peer in peers:
        pl.semaphore_signal(barrier, inc=1, device_id=peer, device_id_type=MESH)
    pl.semaphore_wait(barrier, len(peers))

    def z_copy(up, t, r):
        source = at_z(NZ - t) if up else at_z(t)
        slot = source * BR + r
        side = 0 if up else 1
        return remote(pool.at[slot], pool.at[slot], zs_sem.at[side, t, r], zr_sem.at[side, t, r],
                      dev(y, c, x, at_z(1) if up else at_z(NZ - 1)))

    def z_rows(up, t):
        if t < 3:
            return range(BR)
        return range(0, BR // 2) if up else range(BR // 2, BR)

    def x_copy(q, kind):
        t, up, _ = SOURCES[q]
        zsrc = at_z(NZ - t) if up else at_z(t)
        upward = SOURCES[q][2]
        ahead = 1 if upward else NX - 1
        if kind == 0:
            src, dst, to = stage.at[q, 0], pool.at[NF + x * NZ + zsrc], at_x(1)
        elif kind == 1:
            src, dst, to = stage.at[q, 1], pool.at[NF + x * NZ + zsrc], at_x(NX - 1)
        elif kind == 2:
            src, dst, to = stage.at[q, 2], pool.at[NF + at_x(ahead) * NZ + zsrc], at_x(ahead)
        else:
            src, dst, to = pool.at[NF + x * NZ + zsrc], pool.at[NF + at_x(NX - ahead) * NZ + zsrc], at_x(ahead)
        return remote(src, dst, xs_sem.at[q, kind], xr_sem.at[q, kind], dev(y, c, to, z))

    def pick(q):
        t, up, _ = SOURCES[q]
        zsrc = at_z(NZ - t) if up else at_z(t)
        rows = ROWS // 4
        for kind, d in ((2, 2), (0, 1), (1, NX - 1)):
            chosen = tab[PICK, zsrc * NX + at_x(d)]

            def part(i, carry):
                at = pl.ds(pl.multiple_of(i * rows, rows), rows)
                got = pool[zsrc * BR, at, :]
                for r in range(1, BR):
                    got = jnp.where(chosen == r, pool[zsrc * BR + r, at, :], got)
                stage[q, kind, at, :] = got
                return carry

            lax.fori_loop(0, 4, part, 0)
            x_copy(q, kind).start()

    def relay(q):
        x_copy(q, 2).wait_recv()
        x_copy(q, 3).start()

    for r, load in enumerate(loads):
        load.wait()
        z_copy(True, 0, r).start()
        z_copy(False, 0, r).start()
    pick(0)

    def first(b, carry):
        block = jnp.where(tab[FILLED, b] > 0, prec[b], 0.0)
        turned = block.T
        wt[b] = turned.astype(BF16)
        tile[...] = jnp.where(tab[FLIP, b] > 0, turned, block)
        oc[b] = tile[pl.ds(pl.multiple_of(samp * CH, CH), CH), :]
        return carry

    lax.fori_loop(0, NBK, first, 0)

    for t in range(1, 5):
        for r in range(BR):
            for up in (True, False):
                if r in z_rows(up, t - 1):
                    z_copy(up, t - 1, r).wait_recv()
                    if t < 4 and r in z_rows(up, t):
                        z_copy(up, t, r).start()
        for q in range(len(SOURCES)):
            if SOURCES[q][0] == t:
                pick(q)
        for q in range(len(SOURCES)):
            if SOURCES[q][0] == t - 1:
                relay(q)
    relay(len(SOURCES) - 1)
    for q in range(len(SOURCES)):
        for kind in (0, 1, 3):
            x_copy(q, kind).wait_recv()
    for up in (True, False):
        for t in range(4):
            for r in z_rows(up, t):
                z_copy(up, t, r).wait_send()
    for q in range(len(SOURCES)):
        for kind in range(4):
            x_copy(q, kind).wait_send()

    def gather_slots(b, carry):
        j, k = b // SL, b % SL
        stk[j, :, pl.ds(pl.multiple_of(k * BK, BK), BK)] = pool[tab[POOL, b]]
        return carry

    lax.fori_loop(0, NBK, gather_slots, 0)

    def pair_copy(it, j):
        return remote(ub.at[it, j], sb.at[it, j], bs_sem.at[it, j], br_sem.at[it, j], dev(y, 1 - c, x, z))

    def y_copy(it, j, d):
        return remote(yb.at[it, j, d - 1], yr.at[it, j, d - 1], ys_sem.at[it, j, d - 1], yr_sem.at[it, j, d - 1],
                      dev(at_y(d), c, x, z))

    def pass_on(it, j):
        pair_copy(it, j).wait_recv()
        for d in range(NY):
            yy = at_y(d)
            summed = uf[j, yy] + sb[it, j, yy].astype(F32)
            if d == 0:
                own[j] = summed
            else:
                yb[it, j, d - 1] = summed.astype(BF16)
                y_copy(it, j, d).start()

    def mx_copy(it, d):
        return remote(ms.at[it, at_x(d)], mx.at[it, x], as_sem.at[it, d - 1], ar_sem.at[it, d - 1], dev(y, c, at_x(d), z))

    def mz_copy(it, d):
        return remote(mx.at[it, :, at_z(d)], mz.at[it, z], ms_sem.at[it, d - 1], mr_sem.at[it, d - 1],
                      dev(y, c, x, at_z(d)))

    def gather_y(src, dst, it, d):
        return remote(src, dst.at[samp], gs_sem.at[it, d - 1], gr_sem.at[it, d - 1], dev(at_y(d), c, x, z))

    def gather_c(src, dst, it, d):
        holder = at_y(NY - d) * NC + c if d else samp
        return remote(src if d == 0 else dst.at[holder], dst.at[holder], hs_sem.at[it, d], hr_sem.at[it, d],
                      dev(y, 1 - c, x, z))

    def gather_samp(src, dst, it):
        for d in range(1, NY):
            gather_y(src, dst, it, d).start()
        gather_c(src, dst, it, 0).start()
        dst[samp] = src[...]
        for d in range(1, NY):
            gather_y(src, dst, it, d).wait_recv()
            gather_c(src, dst, it, d).start()
        for d in range(NY):
            gather_c(src, dst, it, d).wait_recv()

    def gather_sent(src, dst, it):
        for d in range(1, NY):
            gather_y(src, dst, it, d).wait_send()
        for d in range(NY):
            gather_c(src, dst, it, d).wait_send()

    def iteration(it, carry):
        def row(j, carry):
            part = ROWS // 4
            weights = wt[pl.ds(pl.multiple_of(j * SL, SL), SL)].reshape(SL * BK, BK)
            for i in range(4):
                projected = jnp.dot(stk[j, i * part:(i + 1) * part, :], weights, preferred_element_type=F32)
                yt[:, i * part:(i + 1) * part] = projected.astype(BF16).T
            vv[...] = jnp.dot(yt[...], stk[j], preferred_element_type=F32)
            for k in range(SL):
                block = vv[:, k * BK:(k + 1) * BK]
                turned = block.T
                if k == 0:
                    block = 0.5 * (block + turned)
                else:
                    block = jnp.where(tab[FLIP, j * SL + k] > 0, turned, block)
                cut = block.reshape(NY, NC, CH, BK)
                even, odd = cut[:, 0], cut[:, 1]
                uf[j, :, k] = jnp.where(c == 0, even, odd)
                ub[it, j, :, k] = jnp.where(c == 0, odd, even).astype(BF16)
            pair_copy(it, j).start()

            @pl.when(j > 0)
            def _():
                pass_on(it, j - 1)

            return carry

        lax.fori_loop(0, BR, row, 0)
        pass_on(it, BR - 1)

        def finish(j, carry):
            total = own[j]
            for d in range(1, NY):
                y_copy(it, j, d).wait_recv()
                total = total + yr[it, j, d - 1].astype(F32)
            uc[pl.ds(pl.multiple_of(j * SL, SL), SL)] = total
            return carry

        lax.fori_loop(0, BR, finish, 0)

        def post(p, carry):
            ms[it, p // NZ, p % NZ] = uc[tab[LINK, p]].astype(BF16)
            return carry

        lax.fori_loop(0, NF, post, 0)
        for d in range(1, NX):
            mx_copy(it, d).start()
        mx[it, x] = ms[it, x]
        for d in range(1, NX):
            mx_copy(it, d).wait_recv()
        for d in range(1, NZ):
            mz_copy(it, d).start()
        mloc[z] = mx[it, :, z]
        for d in range(1, NZ):
            mz_copy(it, d).wait_recv()
            source = at_z(NZ - d)
            mloc[source] = mz[it, source]

        def update(j, carry):
            for k in range(SL):
                b = j * SL + k
                gradient = uc[b]
                if k > 0:
                    peer = tab[PEER, b]
                    mirrored = jnp.where(tab[LOCAL, b] > 0, uc[tab[MATE, b]], mloc[peer // NX, peer % NX].astype(F32))
                    gradient = 0.5 * (gradient + mirrored)
                stepped = oc[b] - STEP * (gradient * (1.0 / (ROWS * NS)))
                result = jnp.where(stepped > 0, jnp.maximum(stepped - SHRINK, 0.0), jnp.minimum(stepped + SHRINK, 0.0))
                if k == 0:
                    rooted = 0.5 * (stepped + jnp.sqrt(stepped * stepped + 4.0 * STEP))
                    across = lax.broadcasted_iota(jnp.int32, (CH, BK), 1)
                    down = lax.broadcasted_iota(jnp.int32, (CH, BK), 0) + samp * CH
                    result = jnp.where(across == down, rooted, result)
                result = jnp.where(tab[FILLED, b] > 0, result, 0.0)
                oc[b] = result
                wc[it, b] = result.astype(BF16)
            return carry

        lax.fori_loop(0, BR, update, 0)

        @pl.when(it < ITERS - 1)
        def _():
            gather_samp(wc.at[it], wg.at[it], it)

            def turn(b, carry):
                block = wg[it, :, b].reshape(BK, BK)
                wt[b] = jnp.where(tab[FLIP, b] > 0, block, block.T)
                return carry

            lax.fori_loop(0, NBK, turn, 0)

        return carry

    lax.fori_loop(0, ITERS, iteration, 0)
    gather_samp(oc, og, ITERS - 1)

    def store(b, carry):
        block = og[:, b].reshape(BK, BK)
        out[b] = jnp.where(tab[FLIP, b] > 0, block.T, block)
        return carry

    lax.fori_loop(0, NBK, store, 0)

    def sent(it, carry):
        for j in range(BR):
            pair_copy(it, j).wait_send()
            for d in range(1, NY):
                y_copy(it, j, d).wait_send()
        for d in range(1, NX):
            mx_copy(it, d).wait_send()
        for d in range(1, NZ):
            mz_copy(it, d).wait_send()

        @pl.when(it < ITERS - 1)
        def _():
            gather_sent(wc.at[it], wg.at[it], it)

        return carry

    lax.fori_loop(0, ITERS, sent, 0)
    gather_sent(oc, og, ITERS - 1)


def tables(col_blocks):
    feat = lax.axis_index("feat")
    cols = col_blocks.reshape(NBK)
    filled = cols >= 0
    place = jnp.arange(NBK, dtype=jnp.int32)
    row_ids = feat * BR + place // SL
    holder = jnp.where(filled, cols // BR, feat)
    inside = jnp.where(filled, cols % BR, 0)
    hx, hz = holder // NZ, holder % NZ
    same_x = hx == feat // NZ
    pool = jnp.where(same_x, hz * BR + inside, NF + holder)
    flip = filled & (cols < row_ids)
    local = filled & (holder == feat)
    pair = (cols[:, None] == row_ids[None, :]) & (cols[None, :] == row_ids[:, None])
    mate = jnp.sum(jnp.where(pair, place[None, :], 0), axis=1)
    linked = (filled & (holder != feat))[None, :] & (holder[None, :] == jnp.arange(NF, dtype=jnp.int32)[:, None])
    link = jnp.sum(jnp.where(linked, place[None, :], 0), axis=1)
    rows = jnp.sum(jnp.where(linked, inside[None, :], 0), axis=1)
    groups = [[xx * NZ + zz for xx in range(NX)] for zz in range(NZ)]
    near = lax.all_gather(rows, "feat", axis_index_groups=groups).reshape(NX, NX, NZ)
    picks = lax.dynamic_index_in_dim(near, feat // NZ, axis=1, keepdims=False).T.reshape(NF)
    return jnp.stack([pool, flip.astype(jnp.int32), local.astype(jnp.int32), mate, hz * NX + hx, filled.astype(jnp.int32),
                      link, picks]).astype(jnp.int32)


def local(samples, precision, col_blocks):
    vmem = pl.BlockSpec(memory_space=pltpu.VMEM)
    piece = (SL, CH, BK)
    dma = pltpu.SemaphoreType.DMA
    result = pl.pallas_call(
        kernel,
        out_shape=jax.ShapeDtypeStruct((NBK, BK, BK), F32),
        in_specs=[pl.BlockSpec(memory_space=pltpu.SMEM), pl.BlockSpec(memory_space=pl.ANY), vmem],
        out_specs=vmem,
        scratch_shapes=[
            pltpu.VMEM((2 * NF, ROWS, BK), BF16),
            pltpu.VMEM((NZ, 3, ROWS, BK), BF16),
            pltpu.VMEM((BR, ROWS, SL * BK), BF16),
            pltpu.VMEM((NBK, BK, BK), BF16),
            pltpu.VMEM((BK, ROWS), BF16),
            pltpu.VMEM((BK, SL * BK), F32),
            pltpu.VMEM((BK, BK), F32),
            pltpu.VMEM((NBK, CH, BK), F32),
            pltpu.VMEM((ITERS, BR, NY) + piece, BF16),
            pltpu.VMEM((BR, NY) + piece, F32),
            pltpu.VMEM((ITERS, BR, NY) + piece, BF16),
            pltpu.VMEM((BR,) + piece, F32),
            pltpu.VMEM((ITERS, BR, NY - 1) + piece, BF16),
            pltpu.VMEM((ITERS, BR, NY - 1) + piece, BF16),
            pltpu.VMEM((NBK, CH, BK), F32),
            pltpu.VMEM((ITERS, NX, NZ, CH, BK), BF16),
            pltpu.VMEM((ITERS, NX, NZ, CH, BK), BF16),
            pltpu.VMEM((ITERS, NZ, NX, CH, BK), BF16),
            pltpu.VMEM((NZ, NX, CH, BK), BF16),
            pltpu.VMEM((ITERS, NBK, CH, BK), BF16),
            pltpu.VMEM((ITERS - 1, NS, NBK, CH, BK), BF16),
            pltpu.VMEM((NS, NBK, CH, BK), F32),
            dma((BR,)),
            dma((2, 4, BR)), dma((2, 4, BR)),
            dma((NZ, 4)), dma((NZ, 4)),
            dma((ITERS, BR)), dma((ITERS, BR)),
            dma((ITERS, BR, NY - 1)), dma((ITERS, BR, NY - 1)),
            dma((ITERS, NX - 1)), dma((ITERS, NX - 1)),
            dma((ITERS, NZ - 1)), dma((ITERS, NZ - 1)),
            dma((ITERS, NY - 1)), dma((ITERS, NY - 1)),
            dma((ITERS, NY)), dma((ITERS, NY)),
        ],
        compiler_params=pltpu.CompilerParams(collective_id=0, has_side_effects=True, vmem_limit_bytes=60 * 2**20),
        name="prox_iterations",
    )(tables(col_blocks), samples, precision.reshape(NBK, BK, BK))
    return result.reshape(BR, SL, BK, BK)


def solution(mesh):
    if mesh.shape["samp"] != NS or mesh.shape["feat"] != NF:
        raise ValueError("unexpected mesh")
    return jax.shard_map(
        local,
        mesh=mesh,
        in_specs=(P("samp", "feat"), P("feat", None, None, None), P("feat", None)),
        out_specs=P("feat", None, None, None),
        check_vma=False,
    )
```

time: 752 us -> 249 us (0.33)
  waiting for transfers between devices: 536 us -> 0 us
  Pallas kernels: 0 us -> 233 us
  local copies, waits for them, and re-layouts: 66.5 us -> 7.05 us
  other arithmetic: 57.6 us -> 0.37 us
  starting transfers between devices: 41.6 us -> 0 us
  matrix products: 33.7 us -> 0 us
  between operations: 13.3 us -> 0.7 us
  blocking collectives: 0 us -> 7.82 us
    all_to_all x4 -> x0, waiting for transfers between devices: 322 us -> none  [the longest x1 186 us: local(): lax.all_to_all(outgoing, 'feat', split_axis=1, concat_axis=1, tiled=True)]
    pallas_call x0 -> x1, Pallas kernels: none -> 233 us  [local(): pl.pallas_call(kernel, out_shape=jax.ShapeDtypeStruct((NBK, BK, BK), F32)...]
    psum x3 -> x0, waiting for transfers between devices: 214 us -> none  [local(): gram_blocks = lax.psum(partial_gram, 'samp') / sample_total]
    gather x14 -> x0, local copies, waits for them, and re-layouts: 53.4 us -> none  [the longest x2 19.9 us: local(): stacked = jnp.take(joined, source_index, axis=1)]
    all_to_all x4 -> x0, starting transfers between devices: 41.1 us -> none  [the longest x3 29 us: local(): lax.all_to_all(mirror_outbound(flat_gram, send_slot, send_has), 'feat', s...]
    select_n x11 -> x2, other arithmetic: 36.9 us -> 0.02 us  [the longest x1 0.01 us: tables(): pool = jnp.where(same_x, hz * BR + inside, NF + holder)]
    dot_general x3 -> x0, matrix products: 33.7 us -> none  [local(): jnp.einsum('rla,rlkb->lkab', projected, stacked, preferred_element_type=j...]
    concatenate x1 -> x0, other arithmetic: 8.94 us -> none  [local(): joined = jnp.concatenate([arrived, xblocks], axis=1)]
  transfers between devices with their start and end apart: 7 -> 0, of which waited for: 7 -> 0; matrix products, arithmetic and copies ran while one was open for 2% -> 0% of each run, Pallas kernels for 0% -> 0%
where the time goes in v1:
time: 249 us
  Pallas kernels  233 us (94%)
  blocking collectives  7.82 us (3%)
  local copies, waits for them, and re-layouts  7.05 us (3%)
    pallas_call x1, Pallas kernels, local(): pl.pallas_call(kernel, out_shape=jax.ShapeDtypeStruct((NBK, BK, BK), F32)...  233 us
    unnamed x1, blocking collectives  7.82 us

profile of v1, /device:TPU:1, one launch (start us, length us, event | category | flops | bytes accessed | tf_op | source)
XLA Modules:
  0.0 249.0 jit_solution(17271812245034729617)
XLA Ops:
  0.0 1.3 dynamic-slice
  1.9 0.8 eq.71
  2.7 0.8 reshape.359
  3.5 0.2 select_reduce_fusion.2
  3.7 0.1 select_reduce_fusion
  3.8 0.2 dynamic-update-slice
  4.1 0.1 reshape.360
  4.2 7.8 %all-reduce.1 = s32[4,4,8]{2,1,0:T(4,128)S(1)} all-reduce(s32[4,4,8]{2,1,0:T(4,128)S(1)} %reshape.360), channel_id=2, replica_groups={{0,8,16,24},{1,9,17,25},{2,10,18,26},{3,11,19,27},{4,12,20,28},{5,13,21..., use_global_device_ids=true, to_apply=%add | all-reduce | flops 128 | bytes 1024
  12.0 0.1 copy.6
  12.1 0.1 stack_reshape.3
  12.2 0.6 stack.16.tab
  12.8 233.1 %prox_iterations.1 = f32[32,128,128]{2,1,0:T(8,128)} custom-call(s32[8,32]{1,0:T(8,128)} %stack.16.tab, bf16[1024,512]{1,0:T(8,128)(2,1)} %x_hbm.1, f32[32,128,128]{2,1,0:T(8,128)} %bitcast.9), custom_call_target="tpu_custom_call" | custom-call | tf_op jit(solution)/shard_map/prox_iterations/pallas_call | solution.py:360
  245.9 3.1 %copy.9 = f32[4,8,128,128]{3,2,1,0:T(8,128)} copy(f32[4,8,128,128]{3,2,1,0:T(8,128)} %bitcast.8) | data formatting | bytes 4194304
  (8 shorter events, 0.1 us)

commit v2 on v1

v2 whole, which is shorter than its diff:
```python
import functools

import jax
import jax.numpy as jnp
from jax import lax
from jax.experimental import pallas as pl
from jax.experimental.pallas import tpu as pltpu
from jax.sharding import PartitionSpec as P

ITERS = 3
STEP = 0.2
SHRINK = 0.2 * 0.25
NX, NZ, NY, NC = 4, 8, 4, 2
NS = NY * NC
NF = NX * NZ
BR, SL, BK = 4, 8, 128
NBK = BR * SL
CH = BK // NS
ROWS = 1024
F32, BF16 = jnp.float32, jnp.bfloat16
MESH = pl.DeviceIdType.MESH

HALF = ROWS // 2

POOL, FLIP, LOCAL, MATE, PEER, FILLED, LINK, PICK = range(8)
SOURCES = ((0, True), (1, True), (1, False), (2, True), (2, False), (3, True), (3, False), (4, True))


def kernel(tab, x_hbm, prec_hbm, out_hbm, pool, stage, stk, wt, yt, vv, tile, prec, oc,
           ub, uf, sb, own, yb, yr, uc, ms, mz, mloc, wc, wg, og, result_rows, loc_sem, out_sem,
           zs_sem, zr_sem, xs_sem, xr_sem, bs_sem, br_sem, ys_sem, yr_sem, ms_sem, mr_sem, gs_sem, gr_sem,
           hs_sem, hr_sem):
    samp, feat = lax.axis_index("samp"), lax.axis_index("feat")
    y, c = samp // NC, samp % NC
    x, z = feat // NZ, feat % NZ

    def at_x(d):
        return (x + d) % NX

    def at_z(d):
        return (z + d) % NZ

    def at_y(d):
        return (y + d) % NY

    def dev(yy, cc, xx, zz):
        return (yy * NC + cc, xx * NZ + zz)

    def remote(src, dst, ssem, rsem, device):
        return pltpu.make_async_remote_copy(src_ref=src, dst_ref=dst, send_sem=ssem, recv_sem=rsem, device_id=device,
                                            device_id_type=MESH)

    barrier = pltpu.get_barrier_semaphore()
    peers = ([dev(y, c, at_x(i // NZ), at_z(i % NZ)) for i in range(1, NF)]
             + [dev(at_y(d), c, x, z) for d in range(1, NY)] + [dev(y, 1 - c, x, z)])
    for peer in peers:
        pl.semaphore_signal(barrier, inc=1, device_id=peer, device_id_type=MESH)
    loads = [pltpu.make_async_copy(x_hbm.at[:, pl.ds(r * BK, BK)], pool.at[z * BR + r], loc_sem.at[r]) for r in range(BR)]
    loads.append(pltpu.make_async_copy(prec_hbm, prec, loc_sem.at[BR]))
    for load in loads:
        load.start()
    pl.semaphore_wait(barrier, len(peers))

    def z_copy(up, t, h, r):
        source = at_z(NZ - t) if up else at_z(t)
        piece = pool.at[source * BR + r, pl.ds(h * HALF, HALF)]
        side = 0 if up else 1
        return remote(piece, piece, zs_sem.at[side, t, h, r], zr_sem.at[side, t, h, r],
                      dev(y, c, x, at_z(1) if up else at_z(NZ - 1)))

    def z_halves(up, t):
        if t < 3:
            return (0, 1)
        return (0,) if up else (1,)

    def x_copy(q, h, e):
        t, up = SOURCES[q]
        zsrc = at_z(NZ - t) if up else at_z(t)
        rows = pl.ds(h * HALF, HALF)
        return remote(stage.at[q, e - 1, rows], pool.at[NF + x * NZ + zsrc, rows], xs_sem.at[q, h, e - 1],
                      xr_sem.at[q, h, e - 1], dev(y, c, at_x(e), z))

    def pick(q, h):
        t, up = SOURCES[q]
        zsrc = at_z(NZ - t) if up else at_z(t)
        rows = HALF // 2
        for e in (2, 1, 3):
            chosen = tab[PICK, zsrc * NX + at_x(e)]

            def part(i, carry):
                at = pl.ds(pl.multiple_of(h * HALF + i * rows, rows), rows)
                got = pool[zsrc * BR, at, :]
                for r in range(1, BR):
                    got = jnp.where(chosen == r, pool[zsrc * BR + r, at, :], got)
                stage[q, e - 1, at, :] = got
                return carry

            lax.fori_loop(0, 2, part, 0)
            x_copy(q, h, e).start()

    for r in range(BR):
        loads[r].wait()
    for h in range(2):
        for r in range(BR):
            z_copy(True, 0, h, r).start()
            z_copy(False, 0, h, r).start()
    for h in range(2):
        pick(0, h)

    def first(b, carry):
        block = jnp.where(tab[FILLED, b] > 0, prec[b], 0.0)
        turned = block.T
        wt[b] = turned.astype(BF16)
        tile[...] = jnp.where(tab[FLIP, b] > 0, turned, block)
        oc[b] = tile[pl.ds(pl.multiple_of(samp * CH, CH), CH), :]
        return carry

    for t in range(1, 5):
        for h in range(2):
            for r in range(BR):
                for up in (True, False):
                    if h in z_halves(up, t - 1):
                        z_copy(up, t - 1, h, r).wait_recv()
                        if t < 4 and h in z_halves(up, t):
                            z_copy(up, t, h, r).start()
            for q in range(len(SOURCES)):
                if SOURCES[q][0] == t:
                    pick(q, h)
            if t == 1 and h == 0:
                loads[BR].wait()
                lax.fori_loop(0, NBK, first, 0)
    for q in range(len(SOURCES)):
        for h in range(2):
            for e in range(1, NX):
                x_copy(q, h, e).wait_recv()
    for up in (True, False):
        for t in range(4):
            for h in z_halves(up, t):
                for r in range(BR):
                    z_copy(up, t, h, r).wait_send()
    for q in range(len(SOURCES)):
        for h in range(2):
            for e in range(1, NX):
                x_copy(q, h, e).wait_send()

    def gather_slots(b, carry):
        j, k = b // SL, b % SL
        stk[j, :, pl.ds(pl.multiple_of(k * BK, BK), BK)] = pool[tab[POOL, b]]
        return carry

    lax.fori_loop(0, NBK, gather_slots, 0)

    last = ITERS - 1

    def pair_copy(it, j):
        return remote(ub.at[it, j], sb.at[it, j], bs_sem.at[it, j], br_sem.at[it, j], dev(y, 1 - c, x, z))

    def y_copy(it, j, d):
        return remote(yb.at[it, j, d - 1], yr.at[it, j, d - 1], ys_sem.at[it, j, d - 1], yr_sem.at[it, j, d - 1],
                      dev(at_y(d), c, x, z))

    def pass_on(it, j):
        pair_copy(it, j).wait_recv()
        for d in (2, 1, 3, 0):
            yy = at_y(d)
            summed = uf[j, yy] + sb[it, j, yy].astype(F32)
            if d == 0:
                own[j] = summed
            else:
                yb[it, j, d - 1] = summed.astype(BF16)
                y_copy(it, j, d).start()

    def mirror_copy(it, i):
        e, d = i // NZ, i % NZ
        return remote(ms.at[it, i], mz.at[it, i], ms_sem.at[it, i], mr_sem.at[it, i], dev(y, c, at_x(e), at_z(d)))

    def piece_of(ref, j):
        return ref.at[pl.ds(pl.multiple_of(j * SL, SL), SL)]

    def gather_y(src, dst, it, j, d):
        return remote(piece_of(src, j), dst.at[j, samp], gs_sem.at[it, j, d - 1], gr_sem.at[it, j, d - 1],
                      dev(at_y(d), c, x, z))

    def gather_c(src, dst, it, j, e):
        holder = at_y(NY - e) * NC + c if e else samp
        source = dst.at[j, holder] if e else piece_of(src, j)
        return remote(source, dst.at[j, holder], hs_sem.at[it, j, e], hr_sem.at[it, j, e], dev(y, 1 - c, x, z))

    def gather_start(src, dst, it, j):
        for d in (2, 1, 3):
            gather_y(src, dst, it, j, d).start()
        gather_c(src, dst, it, j, 0).start()
        dst[j, samp] = src[pl.ds(pl.multiple_of(j * SL, SL), SL)]

    def gather_turn(src, dst, it, j):
        for d in (1, 3, 2):
            gather_y(src, dst, it, j, d).wait_recv()
            gather_c(src, dst, it, j, d).start()

    def gather_done(src, dst, it, j):
        for e in range(NY):
            gather_c(src, dst, it, j, e).wait_recv()

    def gather_sent(src, dst, it):
        def sent(j, carry):
            for d in range(1, NY):
                gather_y(src, dst, it, j, d).wait_send()
            for e in range(NY):
                gather_c(src, dst, it, j, e).wait_send()
            return carry

        lax.fori_loop(0, BR, sent, 0)

    def iteration(it, carry):
        @pl.when(it > 0)
        def _():
            gather_turn(wc.at[it - 1], wg.at[it - 1], it - 1, 0)

        def row(j, carry):
            @pl.when(it > 0)
            def _():
                gather_done(wc.at[it - 1], wg.at[it - 1], it - 1, j)
                for k in range(SL):
                    block = wg[it - 1, j, :, k].reshape(BK, BK)
                    wt[j * SL + k] = jnp.where(tab[FLIP, j * SL + k] > 0, block, block.T)

            part = ROWS // 4
            weights = wt[pl.ds(pl.multiple_of(j * SL, SL), SL)].reshape(SL * BK, BK)
            for i in range(4):
                projected = jnp.dot(stk[j, i * part:(i + 1) * part, :], weights, preferred_element_type=F32)
                yt[:, i * part:(i + 1) * part] = projected.astype(BF16).T
            vv[...] = jnp.dot(yt[...], stk[j], preferred_element_type=F32)

            @pl.when((it > 0) & (j < BR - 1))
            def _():
                gather_turn(wc.at[it - 1], wg.at[it - 1], it - 1, j + 1)

            for k in range(SL):
                block = vv[:, k * BK:(k + 1) * BK]
                turned = block.T
                if k == 0:
                    block = 0.5 * (block + turned)
                else:
                    block = jnp.where(tab[FLIP, j * SL + k] > 0, turned, block)
                cut = block.reshape(NY, NC, CH, BK)
                even, odd = cut[:, 0], cut[:, 1]
                uf[j, :, k] = jnp.where(c == 0, even, odd)
                ub[it, j, :, k] = jnp.where(c == 0, odd, even).astype(BF16)
            pair_copy(it, j).start()

            @pl.when(j > 0)
            def _():
                pass_on(it, j - 1)

            return carry

        lax.fori_loop(0, BR, row, 0)
        pass_on(it, BR - 1)

        def finish(j, carry):
            total = own[j]
            for d in range(1, NY):
                y_copy(it, j, d).wait_recv()
                total = total + yr[it, j, d - 1].astype(F32)
            uc[pl.ds(pl.multiple_of(j * SL, SL), SL)] = total
            return carry

        lax.fori_loop(0, BR, finish, 0)

        def post(i, carry):
            ms[it, i] = uc[tab[LINK, at_x(i // NZ) * NZ + at_z(i % NZ)]].astype(BF16)
            mirror_copy(it, i).start()
            return carry

        lax.fori_loop(1, NF, post, 0)

        def collect(i, carry):
            mirror_copy(it, i).wait_recv()
            mloc[at_z(NZ - i % NZ), at_x(NX - i // NZ)] = mz[it, i]
            return carry

        lax.fori_loop(1, NF, collect, 0)

        def update(j, carry):
            for k in range(SL):
                b = j * SL + k
                gradient = uc[b]
                if k > 0:
                    peer = tab[PEER, b]
                    mirrored = jnp.where(tab[LOCAL, b] > 0, uc[tab[MATE, b]], mloc[peer // NX, peer % NX].astype(F32))
                    gradient = 0.5 * (gradient + mirrored)
                stepped = oc[b] - STEP * (gradient * (1.0 / (ROWS * NS)))
                result = jnp.where(stepped > 0, jnp.maximum(stepped - SHRINK, 0.0), jnp.minimum(stepped + SHRINK, 0.0))
                if k == 0:
                    rooted = 0.5 * (stepped + jnp.sqrt(stepped * stepped + 4.0 * STEP))
                    across = lax.broadcasted_iota(jnp.int32, (CH, BK), 1)
                    down = lax.broadcasted_iota(jnp.int32, (CH, BK), 0) + samp * CH
                    result = jnp.where(across == down, rooted, result)
                result = jnp.where(tab[FILLED, b] > 0, result, 0.0)
                oc[b] = result
                wc[it, b] = result.astype(BF16)

            @pl.when(it < last)
            def _():
                gather_start(wc.at[it], wg.at[it], it, j)

            @pl.when(it == last)
            def _():
                gather_start(oc, og, last, j)

            return carry

        lax.fori_loop(0, BR, update, 0)
        return carry

    lax.fori_loop(0, ITERS, iteration, 0)

    def out_copy(j):
        rows = pl.ds(pl.multiple_of(j * SL, SL), SL)
        return pltpu.make_async_copy(result_rows.at[rows], out_hbm.at[rows], out_sem.at[j])

    gather_turn(oc, og, last, 0)

    def store(j, carry):
        gather_done(oc, og, last, j)
        for k in range(SL):
            block = og[j, :, k].reshape(BK, BK)
            result_rows[j * SL + k] = jnp.where(tab[FLIP, j * SL + k] > 0, block.T, block)
        out_copy(j).start()

        @pl.when(j < BR - 1)
        def _():
            gather_turn(oc, og, last, j + 1)

        return carry

    lax.fori_loop(0, BR, store, 0)

    def sent(it, carry):
        for j in range(BR):
            pair_copy(it, j).wait_send()
            for d in range(1, NY):
                y_copy(it, j, d).wait_send()

        def mirror_sent(i, carry):
            mirror_copy(it, i).wait_send()
            return carry

        lax.fori_loop(1, NF, mirror_sent, 0)

        @pl.when(it < last)
        def _():
            gather_sent(wc.at[it], wg.at[it], it)

        return carry

    lax.fori_loop(0, ITERS, sent, 0)
    gather_sent(oc, og, last)
    for j in range(BR):
        out_copy(j).wait()


def tables(col_blocks):
    feat = lax.axis_index("feat")
    cols = col_blocks.reshape(NBK)
    filled = cols >= 0
    place = jnp.arange(NBK, dtype=jnp.int32)
    row_ids = feat * BR + place // SL
    holder = jnp.where(filled, cols // BR, feat)
    inside = jnp.where(filled, cols % BR, 0)
    hx, hz = holder // NZ, holder % NZ
    same_x = hx == feat // NZ
    pool = jnp.where(same_x, hz * BR + inside, NF + holder)
    flip = filled & (cols < row_ids)
    local = filled & (holder == feat)
    pair = (cols[:, None] == row_ids[None, :]) & (cols[None, :] == row_ids[:, None])
    mate = jnp.sum(jnp.where(pair, place[None, :], 0), axis=1)
    linked = (filled & (holder != feat))[None, :] & (holder[None, :] == jnp.arange(NF, dtype=jnp.int32)[:, None])
    link = jnp.sum(jnp.where(linked, place[None, :], 0), axis=1)
    rows = jnp.sum(jnp.where(linked, inside[None, :], 0), axis=1)
    groups = [[xx * NZ + zz for xx in range(NX)] for zz in range(NZ)]
    near = lax.all_gather(rows, "feat", axis_index_groups=groups).reshape(NX, NX, NZ)
    picks = lax.dynamic_index_in_dim(near, feat // NZ, axis=1, keepdims=False).T.reshape(NF)
    return jnp.stack([pool, flip.astype(jnp.int32), local.astype(jnp.int32), mate, hz * NX + hx, filled.astype(jnp.int32),
                      link, picks]).astype(jnp.int32)


def local(samples, precision, col_blocks):
    anywhere = pl.BlockSpec(memory_space=pl.ANY)
    piece = (SL, CH, BK)
    dma = pltpu.SemaphoreType.DMA
    result = pl.pallas_call(
        kernel,
        out_shape=jax.ShapeDtypeStruct((NBK, BK, BK), F32),
        in_specs=[pl.BlockSpec(memory_space=pltpu.SMEM), anywhere, anywhere],
        out_specs=anywhere,
        scratch_shapes=[
            pltpu.VMEM((2 * NF, ROWS, BK), BF16),
            pltpu.VMEM((NZ, 3, ROWS, BK), BF16),
            pltpu.VMEM((BR, ROWS, SL * BK), BF16),
            pltpu.VMEM((NBK, BK, BK), BF16),
            pltpu.VMEM((BK, ROWS), BF16),
            pltpu.VMEM((BK, SL * BK), F32),
            pltpu.VMEM((BK, BK), F32),
            pltpu.VMEM((NBK, BK, BK), F32),
            pltpu.VMEM((NBK, CH, BK), F32),
            pltpu.VMEM((ITERS, BR, NY) + piece, BF16),
            pltpu.VMEM((BR, NY) + piece, F32),
            pltpu.VMEM((ITERS, BR, NY) + piece, BF16),
            pltpu.VMEM((BR,) + piece, F32),
            pltpu.VMEM((ITERS, BR, NY - 1) + piece, BF16),
            pltpu.VMEM((ITERS, BR, NY - 1) + piece, BF16),
            pltpu.VMEM((NBK, CH, BK), F32),
            pltpu.VMEM((ITERS, NF, CH, BK), BF16),
            pltpu.VMEM((ITERS, NF, CH, BK), BF16),
            pltpu.VMEM((NZ, NX, CH, BK), BF16),
            pltpu.VMEM((ITERS, NBK, CH, BK), BF16),
            pltpu.VMEM((ITERS - 1, BR, NS) + piece, BF16),
            pltpu.VMEM((BR, NS) + piece, F32),
            pltpu.VMEM((NBK, BK, BK), F32),
            dma((BR + 1,)), dma((BR,)),
            dma((2, 4, 2, BR)), dma((2, 4, 2, BR)),
            dma((NZ, 2, NX - 1)), dma((NZ, 2, NX - 1)),
            dma((ITERS, BR)), dma((ITERS, BR)),
            dma((ITERS, BR, NY - 1)), dma((ITERS, BR, NY - 1)),
            dma((ITERS, NF)), dma((ITERS, NF)),
            dma((ITERS, BR, NY - 1)), dma((ITERS, BR, NY - 1)),
            dma((ITERS, BR, NY)), dma((ITERS, BR, NY)),
        ],
        compiler_params=pltpu.CompilerParams(collective_id=0, has_side_effects=True, vmem_limit_bytes=60 * 2**20),
        name="prox_iterations",
    )(tables(col_blocks), samples, precision.reshape(NBK, BK, BK))
    return result.reshape(BR, SL, BK, BK)


def solution(mesh):
    if mesh.shape["samp"] != NS or mesh.shape["feat"] != NF:
        raise ValueError("unexpected mesh")
    return jax.shard_map(
        local,
        mesh=mesh,
        in_specs=(P("samp", "feat"), P("feat", None, None, None), P("feat", None)),
        out_specs=P("feat", None, None, None),
        check_vma=False,
    )
```

time: 249 us -> 214 us (0.86)
  Pallas kernels: 233 us -> 198 us
    pallas_call x1, Pallas kernels: 233 us -> 198 us  [local(): pl.pallas_call(kernel, out_shape=jax.ShapeDtypeStruct((NBK, BK, BK), F32)...]
where the time goes in v2:
time: 214 us; the launch traced here: 213 us
  Pallas kernels  198 us (93%)
  blocking collectives  7.82 us (4%)
  local copies, waits for them, and re-layouts  7.05 us (3%)
    pallas_call x1, Pallas kernels, local(): pl.pallas_call(kernel, out_shape=jax.ShapeDtypeStruct((NBK, BK, BK), F32)...  198 us
    unnamed x1, blocking collectives  7.82 us
    unnamed x4, local copies, waits for them, and re-layouts  4.64 us

profile of v2, /device:TPU:1, one launch (start us, length us, event | category | flops | bytes accessed | tf_op | source)
XLA Modules:
  0.0 213.5 jit_solution(18132280529152396312)
XLA Ops:
  0.0 1.3 dynamic-slice
  1.9 0.8 eq.71
  2.7 0.8 reshape.359
  3.5 0.2 select_reduce_fusion.2
  3.7 0.1 select_reduce_fusion
  3.8 0.2 dynamic-update-slice
  4.1 0.1 reshape.360
  4.2 7.8 %all-reduce.1 = s32[4,4,8]{2,1,0:T(4,128)S(1)} all-reduce(s32[4,4,8]{2,1,0:T(4,128)S(1)} %reshape.360), channel_id=2, replica_groups={{0,8,16,24},{1,9,17,25},{2,10,18,26},{3,11,19,27},{4,12,20,28},{5,13,21..., use_global_device_ids=true, to_apply=%add | all-reduce | flops 128 | bytes 1024
  12.0 0.1 copy.6
  12.1 0.1 stack_reshape.3
  12.2 0.6 stack.16.tab
  12.8 197.5 %prox_iterations.1 = f32[32,128,128]{2,1,0:T(8,128)} custom-call(s32[8,32]{1,0:T(8,128)} %stack.16.tab, bf16[1024,512]{1,0:T(8,128)(2,1)} %x_hbm.1, f32[32,128,128]{2,1,0:T(8,128)} %bitcast.9), custom_call_target="tpu_custom_call" | custom-call | tf_op jit(solution)/shard_map/prox_iterations/pallas_call | solution.py:392
  210.3 3.1 %copy.9 = f32[4,8,128,128]{3,2,1,0:T(8,128)} copy(f32[4,8,128,128]{3,2,1,0:T(8,128)} %bitcast.8) | data formatting | bytes 4194304
  (8 shorter events, 0.1 us)

commit v3 on v2

--- a/solution.py
+++ b/solution.py
@@ -85,7 +85,7 @@
         zsrc = at_z(NZ - t) if up else at_z(t)
         rows = HALF // 2
         for e in (2, 1, 3):
-            chosen = tab[PICK, zsrc * NX + at_x(e)]
+            chosen = tab[PICK, e * NZ + zsrc]
 
             def part(i, carry):
                 at = pl.ds(pl.multiple_of(h * HALF + i * rows, rows), rows)
@@ -174,6 +174,12 @@
         e, d = i // NZ, i % NZ
         return remote(ms.at[it, i], mz.at[it, i], ms_sem.at[it, i], mr_sem.at[it, i], dev(y, c, at_x(e), at_z(d)))
 
+    def far_first(n):
+        kz, kx = n // NX, n % NX
+        d = (NZ // 2 + (kz + 1) // 2 * (2 * (kz % 2) - 1)) % NZ
+        e = (NX // 2 + (kx + 1) // 2 * (2 * (kx % 2) - 1)) % NX
+        return e * NZ + d
+
     def piece_of(ref, j):
         return ref.at[pl.ds(pl.multiple_of(j * SL, SL), SL)]
 
@@ -267,19 +273,21 @@
 
         lax.fori_loop(0, BR, finish, 0)
 
-        def post(i, carry):
+        def post(n, carry):
+            i = far_first(n)
             ms[it, i] = uc[tab[LINK, at_x(i // NZ) * NZ + at_z(i % NZ)]].astype(BF16)
             mirror_copy(it, i).start()
             return carry
 
-        lax.fori_loop(1, NF, post, 0)
-
-        def collect(i, carry):
+        lax.fori_loop(0, NF - 1, post, 0)
+
+        def collect(n, carry):
+            i = far_first(n)
             mirror_copy(it, i).wait_recv()
             mloc[at_z(NZ - i % NZ), at_x(NX - i // NZ)] = mz[it, i]
             return carry
 
-        lax.fori_loop(1, NF, collect, 0)
+        lax.fori_loop(0, NF - 1, collect, 0)
 
         def update(j, carry):
             for k in range(SL):
@@ -378,11 +386,12 @@
     linked = (filled & (holder != feat))[None, :] & (holder[None, :] == jnp.arange(NF, dtype=jnp.int32)[:, None])
     link = jnp.sum(jnp.where(linked, place[None, :], 0), axis=1)
     rows = jnp.sum(jnp.where(linked, inside[None, :], 0), axis=1)
-    groups = [[xx * NZ + zz for xx in range(NX)] for zz in range(NZ)]
-    near = lax.all_gather(rows, "feat", axis_index_groups=groups).reshape(NX, NX, NZ)
-    picks = lax.dynamic_index_in_dim(near, feat // NZ, axis=1, keepdims=False).T.reshape(NF)
-    return jnp.stack([pool, flip.astype(jnp.int32), local.astype(jnp.int32), mate, hz * NX + hx, filled.astype(jnp.int32),
-                      link, picks]).astype(jnp.int32)
+    outgoing = lax.dynamic_slice(jnp.concatenate([rows, rows]), ((feat // NZ) * NZ,), (NF,)).reshape(NX, NZ)
+    come = [lax.ppermute(outgoing[NX - e], "feat", [(xx * NZ + zz, (xx + NX - e) % NX * NZ + zz) for xx in range(NX)
+                                                    for zz in range(NZ)]) for e in range(1, NX)]
+    picks = jnp.concatenate([outgoing[0]] + come)
+    scalars = [pool, flip.astype(jnp.int32), local.astype(jnp.int32), mate, hz * NX + hx, filled.astype(jnp.int32), link, picks]
+    return jnp.concatenate(scalars).reshape(8, NBK)
 
 
 def local(samples, precision, col_blocks):

time: 214 us -> 211 us (0.986)
  blocking collectives: 7.82 us -> 0 us
  starting transfers between devices: 0 us -> 5.65 us
  local copies, waits for them, and re-layouts: 7.05 us -> 4.81 us
    unnamed x1 -> x0, blocking collectives: 7.82 us -> none
    ppermute x0 -> x3, starting transfers between devices: none -> 5.65 us  [tables(): lax.ppermute(outgoing[NX - e], 'feat', [(xx * NZ + zz, (xx + NX - e) % NX...]
    unnamed x4 -> x1, local copies, waits for them, and re-layouts: 4.64 us -> 3.14 us
  transfers between devices with their start and end apart: 0 -> 3, of which waited for: 0 -> 2; matrix products, arithmetic and copies ran while one was open for 0% -> 0% of each run, Pallas kernels for 0% -> 0%
where the time goes in v3:
time: 211 us; the launch traced here: 210 us
  Pallas kernels  198 us (94%)
  starting transfers between devices  5.65 us (3%)
  local copies, waits for them, and re-layouts  4.81 us (2%)
    pallas_call x1, Pallas kernels, local(): pl.pallas_call(kernel, out_shape=jax.ShapeDtypeStruct((NBK, BK, BK), F32)...  198 us
    ppermute x3, starting transfers between devices, tables(): lax.ppermute(outgoing[NX - e], 'feat', [(xx * NZ + zz, (xx + NX - e) % NX...  5.65 us
  transfers between devices with their start and end apart: 3, of which 2 were waited for; matrix products, arithmetic and copies ran while one was open for 0% of the time, Pallas kernels for 0%

profile of v3, /device:TPU:1, one launch (start us, length us, event | category | flops | bytes accessed | tf_op | source)
XLA Modules:
  0.0 210.4 jit_solution(8455544899981807337)
XLA Ops:
  0.0 0.8 reshape.121
  0.8 0.1 select_reduce_fusion
  0.9 0.1 pad_add_fusion
  1.0 0.1 dynamic_slice.3
  1.1 0.1 fusion.10
  1.2 2.0 collective-permute-start.2
  3.2 2.5 %collective-permute-start.1 = (s32[8]{0:T(128)S(1)}, s32[8]{0:T(128)S(1)}, u32[]{:S(2)}, u32[]{:S(2)}) collective-permute-start(s32[8]{0:T(128)S(1)} %get-tuple-element.15), channel_id=1, source_target_pairs={{0,16},{1,17},{2,18},{3,19},{4,20},{5,21},{6,22},{7,23},{8,24},{9,... | collective-permute-start | bytes 104 | tf_op jit(solution)/shard_map/ppermute | solution.py:390
  5.7 1.2 collective-permute-start
  6.8 0.2 select_reduce_fusion.2
  7.0 0.0 collective-permute-done.2
  7.0 0.1 collective-permute-done.1
  7.1 0.9 collective-permute-done
  8.1 0.1 concatenate.7
  8.1 0.7 reshape.122.tab
  8.8 198.4 %prox_iterations.1 = f32[32,128,128]{2,1,0:T(8,128)} custom-call(s32[8,32]{1,0:T(8,128)} %reshape.122.tab, bf16[1024,512]{1,0:T(8,128)(2,1)} %x_hbm.1, f32[32,128,128]{2,1,0:T(8,128)} %bitcast.3), custom_call_target="tpu_custom_call" | custom-call | tf_op jit(solution)/shard_map/prox_iterations/pallas_call | solution.py:401
  207.3 3.1 %copy.5 = f32[4,8,128,128]{3,2,1,0:T(8,128)} copy(f32[4,8,128,128]{3,2,1,0:T(8,128)} %bitcast.2) | data formatting | bytes 4194304
  (5 shorter events, 0.1 us)
Async XLA Ops:
  1.2 5.8 %collective-permute-start.2 = (s32[8]{0:T(128)S(1)}, s32[8]{0:T(128)S(1)}, u32[]{:S(2)}, u32[]{:S(2)}) collective-permute-start(s32[8]{0:T(128)S(1)} %get-tuple-element.14), channel_id=1, source_target_pairs={{0,8},{1,9},{2,10},{3,11},{4,12},{5,13},{6,14},{7,15},{8,16},{9,17... | collective-permute-start | bytes 104 | tf_op jit(solution)/shard_map/ppermute | solution.py:390
  3.2 3.9 %collective-permute-start.1 = (s32[8]{0:T(128)S(1)}, s32[8]{0:T(128)S(1)}, u32[]{:S(2)}, u32[]{:S(2)}) collective-permute-start(s32[8]{0:T(128)S(1)} %get-tuple-element.15), channel_id=1, source_target_pairs={{0,16},{1,17},{2,18},{3,19},{4,20},{5,21},{6,22},{7,23},{8,24},{9,... | collective-permute-start | bytes 104 | tf_op jit(solution)/shard_map/ppermute | solution.py:390
  5.7 2.4 %collective-permute-start = (s32[8]{0:T(128)S(1)}, s32[8]{0:T(128)S(1)}, u32[]{:S(2)}, u32[]{:S(2)}) collective-permute-start(s32[8]{0:T(128)S(1)} %get-tuple-element.16), channel_id=1, source_target_pairs={{0,24},{1,25},{2,26},{3,27},{4,28},{5,29},{6,30},{7,31},{8,0},{9,1... | collective-permute-start | bytes 104 | tf_op jit(solution)/shard_map/ppermute | solution.py:390

commit v4 on v3

--- a/solution.py
+++ b/solution.py
@@ -20,7 +20,8 @@
 F32, BF16 = jnp.float32, jnp.bfloat16
 MESH = pl.DeviceIdType.MESH
 
-HALF = ROWS // 2
+PIECES = 4
+HALF = ROWS // PIECES
 
 POOL, FLIP, LOCAL, MATE, PEER, FILLED, LINK, PICK = range(8)
 SOURCES = ((0, True), (1, True), (1, False), (2, True), (2, False), (3, True), (3, False), (4, True))
@@ -70,8 +71,8 @@
 
     def z_halves(up, t):
         if t < 3:
-            return (0, 1)
-        return (0,) if up else (1,)
+            return range(PIECES)
+        return range(0, PIECES // 2) if up else range(PIECES // 2, PIECES)
 
     def x_copy(q, h, e):
         t, up = SOURCES[q]
@@ -100,11 +101,11 @@
 
     for r in range(BR):
         loads[r].wait()
-    for h in range(2):
+    for h in range(PIECES):
         for r in range(BR):
             z_copy(True, 0, h, r).start()
             z_copy(False, 0, h, r).start()
-    for h in range(2):
+    for h in range(PIECES):
         pick(0, h)
 
     def first(b, carry):
@@ -116,7 +117,7 @@
         return carry
 
     for t in range(1, 5):
-        for h in range(2):
+        for h in range(PIECES):
             for r in range(BR):
                 for up in (True, False):
                     if h in z_halves(up, t - 1):
@@ -130,7 +131,7 @@
                 loads[BR].wait()
                 lax.fori_loop(0, NBK, first, 0)
     for q in range(len(SOURCES)):
-        for h in range(2):
+        for h in range(PIECES):
             for e in range(1, NX):
                 x_copy(q, h, e).wait_recv()
     for up in (True, False):
@@ -139,7 +140,7 @@
                 for r in range(BR):
                     z_copy(up, t, h, r).wait_send()
     for q in range(len(SOURCES)):
-        for h in range(2):
+        for h in range(PIECES):
             for e in range(1, NX):
                 x_copy(q, h, e).wait_send()
 
@@ -428,8 +429,8 @@
             pltpu.VMEM((BR, NS) + piece, F32),
             pltpu.VMEM((NBK, BK, BK), F32),
             dma((BR + 1,)), dma((BR,)),
-            dma((2, 4, 2, BR)), dma((2, 4, 2, BR)),
-            dma((NZ, 2, NX - 1)), dma((NZ, 2, NX - 1)),
+            dma((2, 4, PIECES, BR)), dma((2, 4, PIECES, BR)),
+            dma((NZ, PIECES, NX - 1)), dma((NZ, PIECES, NX - 1)),
             dma((ITERS, BR)), dma((ITERS, BR)),
             dma((ITERS, BR, NY - 1)), dma((ITERS, BR, NY - 1)),
             dma((ITERS, NF)), dma((ITERS, NF)),

time: 211 us -> 214 us (1.014)
  Pallas kernels: 198 us -> 202 us
    pallas_call x1, Pallas kernels: 198 us -> 202 us  [local(): pl.pallas_call(kernel, out_shape=jax.ShapeDtypeStruct((NBK, BK, BK), F32)...]
where the time goes in v4:
time: 214 us
  Pallas kernels  202 us (94%)
  starting transfers between devices  5.65 us (3%)
  local copies, waits for them, and re-layouts  4.81 us (2%)
    pallas_call x1, Pallas kernels, local(): pl.pallas_call(kernel, out_shape=jax.ShapeDtypeStruct((NBK, BK, BK), F32)...  202 us
    ppermute x3, starting transfers between devices, tables(): lax.ppermute(outgoing[NX - e], 'feat', [(xx * NZ + zz, (xx + NX - e) % NX...  5.65 us
  transfers between devices with their start and end apart: 3, of which 2 were waited for; matrix products, arithmetic and copies ran while one was open for 0% of the time, Pallas kernels for 0%

profile of v4, /device:TPU:1, one launch (start us, length us, event | category | flops | bytes accessed | tf_op | source)
XLA Modules:
  0.0 213.5 jit_solution(6379780520466367997)
XLA Ops:
  0.0 0.8 reshape.121
  0.8 0.1 select_reduce_fusion
  0.9 0.1 pad_add_fusion
  1.0 0.1 dynamic_slice.3
  1.1 0.1 fusion.10
  1.2 2.0 collective-permute-start.2
  3.2 2.5 %collective-permute-start.1 = (s32[8]{0:T(128)S(1)}, s32[8]{0:T(128)S(1)}, u32[]{:S(2)}, u32[]{:S(2)}) collective-permute-start(s32[8]{0:T(128)S(1)} %get-tuple-element.15), channel_id=1, source_target_pairs={{0,16},{1,17},{2,18},{3,19},{4,20},{5,21},{6,22},{7,23},{8,24},{9,... | collective-permute-start | bytes 104 | tf_op jit(solution)/shard_map/ppermute | solution.py:391
  5.7 1.2 collective-permute-start
  6.8 0.2 select_reduce_fusion.2
  7.0 0.0 collective-permute-done.2
  7.0 0.1 collective-permute-done.1
  7.1 0.9 collective-permute-done
  8.1 0.1 concatenate.7
  8.1 0.7 reshape.122.tab
  8.8 201.6 %prox_iterations.1 = f32[32,128,128]{2,1,0:T(8,128)} custom-call(s32[8,32]{1,0:T(8,128)} %reshape.122.tab, bf16[1024,512]{1,0:T(8,128)(2,1)} %x_hbm.1, f32[32,128,128]{2,1,0:T(8,128)} %bitcast.3), custom_call_target="tpu_custom_call" | custom-call | tf_op jit(solution)/shard_map/prox_iterations/pallas_call | solution.py:402
  210.4 3.1 %copy.5 = f32[4,8,128,128]{3,2,1,0:T(8,128)} copy(f32[4,8,128,128]{3,2,1,0:T(8,128)} %bitcast.2) | data formatting | bytes 4194304
  (5 shorter events, 0.1 us)
Async XLA Ops:
  1.2 5.8 %collective-permute-start.2 = (s32[8]{0:T(128)S(1)}, s32[8]{0:T(128)S(1)}, u32[]{:S(2)}, u32[]{:S(2)}) collective-permute-start(s32[8]{0:T(128)S(1)} %get-tuple-element.14), channel_id=1, source_target_pairs={{0,8},{1,9},{2,10},{3,11},{4,12},{5,13},{6,14},{7,15},{8,16},{9,17... | collective-permute-start | bytes 104 | tf_op jit(solution)/shard_map/ppermute | solution.py:391
  3.2 3.9 %collective-permute-start.1 = (s32[8]{0:T(128)S(1)}, s32[8]{0:T(128)S(1)}, u32[]{:S(2)}, u32[]{:S(2)}) collective-permute-start(s32[8]{0:T(128)S(1)} %get-tuple-element.15), channel_id=1, source_target_pairs={{0,16},{1,17},{2,18},{3,19},{4,20},{5,21},{6,22},{7,23},{8,24},{9,... | collective-permute-start | bytes 104 | tf_op jit(solution)/shard_map/ppermute | solution.py:391
  5.7 2.4 %collective-permute-start = (s32[8]{0:T(128)S(1)}, s32[8]{0:T(128)S(1)}, u32[]{:S(2)}, u32[]{:S(2)}) collective-permute-start(s32[8]{0:T(128)S(1)} %get-tuple-element.16), channel_id=1, source_target_pairs={{0,24},{1,25},{2,26},{3,27},{4,28},{5,29},{6,30},{7,31},{8,0},{9,1... | collective-permute-start | bytes 104 | tf_op jit(solution)/shard_map/ppermute | solution.py:391
